TPU v7x, 128 devices: a whole 4x4x4 slice. The times are simulated.
128 devices in a mesh: req: 16 (over z, y), kv: 8 (over x, core).
Axes of the slice: x: 4, y: 4, z: 4, core: 2. Of those that a mesh axis runs over, the one named last changes fastest.
Arguments:
- hidden_in: bfloat16 [16384, 2048], P(('req', 'kv')), may hold values from -6 to 6
- slot_tokens: int32 [16384], replicated, may hold values from 0 to 16383, as said below
- cache_len: int32 [128], P('req'), may hold values from 1 to 2048, 65536 in all
- prefill_start: int32 [16], P('req'), may hold values from 0 to 2048
- key_cache: bfloat16 [128, 2048, 1024], P('req', None, 'kv')
- value_cache: bfloat16 [128, 2048, 1024], P('req', None, 'kv'), may hold values from -18 to 18
- key_prefix: bfloat16 [16, 2048, 1024], P('req', None, 'kv')
- value_prefix: bfloat16 [16, 2048, 1024], P('req', None, 'kv'), may hold values from -18 to 18
- attn_gain: float32 [2048], replicated, may hold values from 0.25 to 1.75
- q_proj: bfloat16 [2048, 2048], P(None, 'kv'), may hold values from -0.125 to 0.125
- k_proj: bfloat16 [2048, 1024], P(None, 'kv'), may hold values from -0.125 to 0.125
- v_proj: bfloat16 [2048, 1024], P(None, 'kv'), may hold values from -0.125 to 0.125
- q_gain: float32 [128], replicated, may hold values from 0.25 to 1.75
- k_gain: float32 [128], replicated, may hold values from 0.25 to 1.75
- o_proj: bfloat16 [2048, 2048], P('kv'), may hold values from -0.125 to 0.125
- ffn_gain: float32 [2048], replicated, may hold values from 0.25 to 1.75
- w_gate: bfloat16 [2048, 6144], P(None, 'req'), may hold values from -0.125 to 0.125
- w_up: bfloat16 [2048, 6144], P(None, 'req'), may hold values from -0.125 to 0.125
- w_down: bfloat16 [6144, 2048], P('req'), may hold values from -0.078125 to 0.078125
- final_gain: float32 [2048], replicated, may hold values from 0.25 to 1.75
- lm_head: bfloat16 [2048, 151936], P(None, ('req', 'kv')), may hold values from -0.375 to 0.375
Outputs:
- layer_out: bfloat16 [16384, 2048], P(('req', 'kv'))
- max_logit: float32 [144], replicated
Inputs may be any that keep to these rules, and one draw needn't show every extreme that they name: slot_tokens is a permutation of the batch's tokens; each device's 128 consecutive slots take exactly 1 token from each device's 128 consecutive batch tokens.
All inputs are finite; a program needn't handle non-finite values. No bound on the sum of `cache_len` on one device may be relied on, other than what follows from the above.
Results may differ from a plain program's by a relative error of at most 0.0085.
The roundings to bfloat16 on the way count: a program that leaves them out, or rounds other values in their place, can miss the bound.
Values may be sent and summed in bfloat16 or wider, within the bound.
A program may use at most 128 MiB of HBM per device.

v0:
```python
import jax
import jax.numpy as jnp
from jax import lax
from jax.sharding import PartitionSpec as P

EPS = 1e-06
NEG = -1e30


def spread(value, axis, root):
    mine = lax.axis_index(axis) == root
    return lax.psum(jnp.where(mine, value, jnp.zeros_like(value)), axis)


def norm_rows(values, gain_vec):
    wide = values.astype(jnp.float32)
    return wide * lax.rsqrt(jnp.mean(wide * wide, axis=-1, keepdims=True) + EPS) * gain_vec


def rotate(values, places):
    half_dim = values.shape[-1] // 2
    freqs = 1000000.0 ** (-(jnp.arange(half_dim, dtype=jnp.float32) * 2.0 / values.shape[-1]))
    angles = places[:, None] * freqs[None, :]
    cosine = jnp.cos(angles)[:, None, :]
    sine = jnp.sin(angles)[:, None, :]
    first_half = values[..., :half_dim]
    second_half = values[..., half_dim:]
    return jnp.concatenate(
        [first_half * cosine - second_half * sine, second_half * cosine + first_half * sine],
        axis=-1,
    )


def prefill_full(q_heads, key_old, value_old, key_new, value_new, start_at):
    old_len = key_old.shape[0]
    fresh_rows = q_heads.shape[0]
    factor = q_heads.shape[-1] ** (-0.5)
    all_keys = jnp.concatenate([key_old, key_new], axis=0)
    all_values = jnp.concatenate([value_old, value_new], axis=0)
    scores = (
        jnp.einsum("cgd,kd->gck", q_heads, all_keys, preferred_element_type=jnp.float32) * factor
    )
    key_index = jnp.arange(old_len + fresh_rows, dtype=jnp.int32)[None, :]
    row_index = jnp.arange(fresh_rows, dtype=jnp.int32)[:, None]
    allowed = jnp.where(key_index < old_len, key_index < start_at, key_index - old_len <= row_index)
    scores = jnp.where(allowed[None], scores, NEG)
    row_peak = jnp.max(scores, axis=-1, keepdims=True)
    expd = jnp.exp(scores - row_peak)
    weights = (expd / jnp.sum(expd, axis=-1, keepdims=True)).astype(jnp.bfloat16)
    return jnp.einsum(
        "gck,kd->cgd", weights, all_values, preferred_element_type=jnp.float32
    ).astype(jnp.bfloat16)


def decode_attend(q_heads, key_old, value_old, key_self, value_self, lengths):
    factor = q_heads.shape[-1] ** (-0.5)
    past = jnp.einsum("bgd,bld->bgl", q_heads, key_old, preferred_element_type=jnp.float32) * factor
    slot_index = jnp.arange(key_old.shape[1], dtype=jnp.int32)
    past = jnp.where(slot_index[None, None, :] < lengths[:, None, None], past, NEG)
    own_score = (
        jnp.einsum("bgd,bd->bg", q_heads, key_self, preferred_element_type=jnp.float32) * factor
    )
    row_peak = jnp.maximum(jnp.max(past, axis=-1), own_score)
    past_exp = jnp.exp(past - row_peak[..., None])
    own_exp = jnp.exp(own_score - row_peak)
    row_total = jnp.sum(past_exp, axis=-1) + own_exp
    past_w = (past_exp / row_total[..., None]).astype(jnp.bfloat16)
    own_w = (own_exp / row_total).astype(jnp.bfloat16)
    summed = jnp.einsum("bgl,bld->bgd", past_w, value_old, preferred_element_type=jnp.float32)
    summed = (
        summed + own_w.astype(jnp.float32)[..., None] * value_self.astype(jnp.float32)[:, None, :]
    )
    return summed.astype(jnp.bfloat16)


def butterfly(value, axis, combine):
    size = lax.axis_size(axis)
    step = 1
    while step < size:
        pairs = [(i, i ^ step) for i in range(size)]
        value = combine(value, lax.ppermute(value, axis, pairs))
        step *= 2
    return value


def butterfly_gather(value, axis):
    size = lax.axis_size(axis)
    me = lax.axis_index(axis)
    step = 1
    while step < size:
        pairs = [(i, i ^ step) for i in range(size)]
        other = lax.ppermute(value, axis, pairs)
        low = me // step % 2 == 0
        value = jnp.concatenate(
            [jnp.where(low, value, other), jnp.where(low, other, value)], axis=0
        )
        step *= 2
    return value


def radix_exchange(value, axis, step, radix):
    size = lax.axis_size(axis)
    got = [value]
    for digit in range(1, radix):
        pairs = [(i, i ^ digit * step) for i in range(size)]
        got.append(lax.ppermute(value, axis, pairs))
    return got


def radix_reduce(value, axis, combine, radix):
    size = lax.axis_size(axis)
    step = 1
    while step < size:
        for other in radix_exchange(value, axis, step, radix)[1:]:
            value = combine(value, other)
        step *= radix
    return value


def radix_gather(value, axis, radix):
    size = lax.axis_size(axis)
    me = lax.axis_index(axis)
    step = 1
    while step < size:
        got = radix_exchange(value, axis, step, radix)
        order = jnp.arange(radix, dtype=jnp.int32) ^ me // step % radix
        value = jnp.stack(got)[order].reshape((radix * value.shape[0],) + value.shape[1:])
        step *= radix
    return value


def mixed_reduce(value, axis, combine, radices):
    me = lax.axis_index(axis)
    step = 1
    for radix in radices:
        got = radix_exchange(value, axis, step, radix)
        order = jnp.arange(radix, dtype=jnp.int32) ^ me // step % radix
        members = jnp.stack(got)[order]
        while members.shape[0] > 1:
            members = combine(members[0::2], members[1::2])
        value = members[0]
        step *= radix
    return value


def regroup(rows_in):
    return lax.all_to_all(rows_in, ("req", "kv"), split_axis=0, concat_axis=0, tiled=True)


def shards(
    hidden_in,
    slot_tokens,
    cache_len,
    prefill_start,
    key_cache,
    value_cache,
    key_prefix,
    value_prefix,
    attn_gain,
    q_proj,
    k_proj,
    v_proj,
    q_gain,
    k_gain,
    o_proj,
    ffn_gain,
    w_gate,
    w_up,
    w_down,
    final_gain,
    lm_head,
):
    req_count = lax.axis_size("req")
    kv_count = lax.axis_size("kv")
    devices = req_count * kv_count
    rows_dev = hidden_in.shape[0]
    kv_index = lax.axis_index("kv")
    self_index = lax.axis_index("req") * kv_count + kv_index
    slot_table = slot_tokens.reshape(devices, rows_dev)
    from_self = slot_table // rows_dev == self_index
    send_rows = jnp.sum(jnp.where(from_self, slot_table - self_index * rows_dev, 0), axis=1)
    slot_place = lax.dynamic_index_in_dim(slot_table, self_index, 0, keepdims=False) // rows_dev
    arrived = regroup(hidden_in[send_rows])
    owner_rows = arrived[slot_place]
    rows_all = lax.all_gather(owner_rows, "kv", axis=0, tiled=True)
    normed = norm_rows(rows_all, attn_gain).astype(jnp.bfloat16)
    o_full = lax.all_to_all(
        jnp.broadcast_to(o_proj[None], (kv_count,) + o_proj.shape),
        "kv",
        split_axis=0,
        concat_axis=0,
        tiled=True,
    ).reshape(kv_count * o_proj.shape[0], o_proj.shape[1])
    ff_dev = w_gate.shape[1]
    ff_piece = ff_dev // kv_count
    weight_piece = jnp.stack(
        [
            lax.dynamic_slice_in_dim(w_gate, kv_index * ff_piece, ff_piece, axis=1).T,
            lax.dynamic_slice_in_dim(w_up, kv_index * ff_piece, ff_piece, axis=1).T,
            lax.dynamic_slice_in_dim(w_down, kv_index * ff_piece, ff_piece, axis=0),
        ]
    )
    weight_all = lax.all_gather(weight_piece, "req", axis=1, tiled=True)
    model_dim = w_gate.shape[0]
    q_cols = q_proj.shape[1]
    kv_cols = k_proj.shape[1]
    projected = jnp.concatenate(
        [
            jnp.dot(normed, q_proj, preferred_element_type=jnp.float32),
            jnp.dot(normed, k_proj, preferred_element_type=jnp.float32),
            jnp.dot(normed, v_proj, preferred_element_type=jnp.float32),
        ],
        axis=1,
    )
    tok_req = projected.shape[0]
    head_dim = q_gain.shape[0]
    dec_count = cache_len.shape[0]
    fresh_count = tok_req - dec_count
    q_raw = projected[:, :q_cols].reshape(tok_req, q_cols // head_dim, head_dim)
    k_raw = projected[:, q_cols : q_cols + kv_cols].reshape(tok_req, kv_cols // head_dim, head_dim)
    v_new = (
        projected[:, q_cols + kv_cols :]
        .astype(jnp.bfloat16)
        .reshape(tok_req, kv_cols // head_dim, head_dim)
    )
    places = jnp.concatenate(
        [prefill_start[0] + jnp.arange(fresh_count, dtype=jnp.int32), cache_len]
    ).astype(jnp.float32)
    queries = rotate(norm_rows(q_raw, q_gain), places).astype(jnp.bfloat16)
    keys_new = rotate(norm_rows(k_raw, k_gain), places).astype(jnp.bfloat16)
    pre_out = prefill_full(
        queries[:fresh_count],
        key_prefix[0, :, 0:head_dim],
        value_prefix[0, :, 0:head_dim],
        keys_new[:fresh_count, 0],
        v_new[:fresh_count, 0],
        prefill_start[0],
    )
    dec_out = decode_attend(
        queries[fresh_count:],
        key_cache,
        value_cache,
        keys_new[fresh_count:, 0],
        v_new[fresh_count:, 0],
        cache_len,
    )
    pieces = jnp.concatenate([pre_out, dec_out], axis=0)
    pieces, weight_all, o_full = lax.optimization_barrier((pieces, weight_all, o_full))
    gate_w = weight_all[0]
    up_w = weight_all[1]
    down_w = weight_all[2]
    attended = lax.all_gather(pieces.reshape(tok_req, q_cols), "kv", axis=1, tiled=True)
    resid = (
        rows_all.astype(jnp.float32) + jnp.dot(attended, o_full, preferred_element_type=jnp.float32)
    ).astype(jnp.bfloat16)
    ffn_in = norm_rows(resid, ffn_gain).astype(jnp.bfloat16)
    contract_last = (((1,), (1,)), ((), ()))
    gate_part = lax.dot_general(ffn_in, gate_w, contract_last, preferred_element_type=jnp.float32)
    up_part = lax.dot_general(ffn_in, up_w, contract_last, preferred_element_type=jnp.float32)
    hidden_act = (jax.nn.silu(gate_part) * up_part).astype(jnp.bfloat16)
    tail_count = tok_req - fresh_count + 1
    tail_pad = -(-tail_count // 8) * 8
    down_part = jnp.dot(hidden_act, down_w, preferred_element_type=jnp.float32)
    ffn_part = lax.psum_scatter(down_part, "kv", scatter_dimension=0, tiled=True)
    tail_part = jnp.dot(
        hidden_act[tok_req - tail_pad :], down_w, preferred_element_type=jnp.float32
    )
    tail_sum = mixed_reduce(tail_part, "kv", jnp.add, (2, 4))[tail_pad - tail_count :]
    tail_out = (resid[fresh_count - 1 :].astype(jnp.float32) + tail_sum).astype(jnp.bfloat16)
    tail_rows = norm_rows(tail_out, final_gain).astype(jnp.bfloat16)
    local_peaks = jnp.max(
        jnp.dot(radix_gather(tail_rows, "req", 4), lm_head, preferred_element_type=jnp.float32),
        axis=1,
    )
    max_logit = radix_reduce(
        mixed_reduce(local_peaks, "kv", jnp.maximum, (2, 4)), "req", jnp.maximum, 4
    )
    ffn_part, max_logit = lax.optimization_barrier((ffn_part, max_logit))
    mine = lax.dynamic_slice_in_dim(resid, kv_index * rows_dev, rows_dev, axis=0)
    out_rows = (mine.astype(jnp.float32) + ffn_part).astype(jnp.bfloat16)
    going_back = jnp.zeros_like(out_rows).at[slot_place].set(out_rows)
    returned = regroup(going_back)
    layer_out = jnp.zeros_like(hidden_in).at[send_rows].set(returned)
    return (layer_out, max_logit)


def solution(mesh):
    placed = (
        P(("req", "kv"), None),
        P(),
        P("req"),
        P("req"),
        P("req", None, "kv"),
        P("req", None, "kv"),
        P("req", None, "kv"),
        P("req", None, "kv"),
        P(),
        P(None, "kv"),
        P(None, "kv"),
        P(None, "kv"),
        P(),
        P(),
        P("kv", None),
        P(),
        P(None, "req"),
        P(None, "req"),
        P("req", None),
        P(),
        P(None, ("req", "kv")),
    )
    return jax.shard_map(
        shards, mesh=mesh, in_specs=placed, out_specs=(P(("req", "kv"), None), P()), check_vma=False
    )
```

profile of v0, /device:TPU:1, one launch (start us, length us, event | category | flops | bytes accessed | tf_op | source)
XLA Modules:
  0.0 336.4 jit_solution(1163954709671219122)
XLA Ops:
  13.5 11.5 %all-to-all-start = ((bf16[128,2,1024]{2,1,0:T(2,128)(2,1)}), bf16[128,2,1024]{2,1,0:T(2,128)(2,1)S(1)}, u32[]{:S(2)}, u32[]{:S(2)}) async-start(bf16[128,2,1024]{2,1,0:T(2,128)(2,1)} %reshape.574), calls=%async_computation | async-start | bytes 1048576 | tf_op jit(solution)/shard_map/all_to_all | solution.py:147
  25.8 13.0 %all-to-all-done = bf16[128,2,1024]{2,1,0:T(2,128)(2,1)S(1)} async-done(((bf16[128,2,1024]{2,1,0:T(2,128)(2,1)}), bf16[128,2,1024]{2,1,0:T(2,128)(2,1)S(1)}, u32[]{:S(2)}, u32[]{:S(2)}) %all-to-all-start) | async-done | bytes 524320 | tf_op jit(solution)/shard_map/all_to_all | solution.py:147
  44.6 5.6 %broadcast_in_dim.46 = bf16[8,256,2048]{2,1,0:T(8,128)(2,1)} broadcast(bf16[256,2048]{1,0:T(8,128)(2,1)} %param.35), dimensions={1,2} | broadcast | bytes 9437184 | tf_op jit(solution)/shard_map/broadcast_in_dim | solution.py:188
  50.2 5.8 %all-to-all-start.1 = ((bf16[8,256,2048]{2,1,0:T(8,128)(2,1)}), bf16[8,256,2048]{2,1,0:T(8,128)(2,1)}, u32[]{:S(2)}, u32[]{:S(2)}) async-start(bf16[8,256,2048]{2,1,0:T(8,128)(2,1)} %broadcast_in_dim.46), calls=%async_computation.1 | async-start | bytes 16777216 | tf_op jit(solution)/shard_map/all_to_all | solution.py:187
  59.0 4.0 %fusion.4 = pred[1016,3064]{1,0:T(8,128)(4,1)} fusion(s32[3064]{0:T(1024)S(1)} %iota_add_fusion, pred[3064]{0:T(1024)(128)(4,1)S(1)} %get-tuple-element.34, pred[3064]{0:T(1024)(128)(4,1)S(1)} %get-tuple-element.35), kind=kLoop, calls=%fused_computation.21 | loop fusion | flops 6226048 | bytes 3131408 | tf_op jit(solution)/shard_map/jit(_where)/select_n | solution.py:45
  63.1 23.5 %all-gather.9.cloned.1.call-done = bf16[1024,2048]{1,0:T(8,128)(2,1)} async-done(((bf16[128,2048]{1,0:T(8,128)(2,1)}), bf16[1024,2048]{1,0:T(8,128)(2,1)}) %all-gather.9.cloned.1.call-update) | async-done | bytes 4194320 | tf_op jit(solution)/shard_map/all_gather | solution.py:185
  86.6 3.2 fusion.10
  95.2 3.7 %multiply_reduce_fusion.1 = (f32[1024]{0:T(1024)S(1)}, f32[1024,128]{0,1:T(8,128)S(1)}) fusion(bf16[1024,2048]{1,0:T(8,128)(2,1)} %copy-done.3, bf16[2048,128]{1,0:T(8,128)(2,1)S(1)} %copy-done.6), kind=kOutput, calls=%fused_computation.77 | convolution fusion | flops 537132032 | bytes 5246976 | tf_op jit(solution)/shard_map/dot_general | solution.py:210
  104.7 3.9 %convolution_convert_fusion = bf16[1024,128]{1,0:T(8,128)(2,1)S(1)} fusion(bf16[1024,2048]{1,0:T(8,128)(2,1)} %copy-done.3, bf16[2048,128]{1,0:T(8,128)(2,1)S(1)} %copy-done.14), kind=kOutput, calls=%fused_computation.51 | convolution fusion | flops 537001984 | bytes 4980736 | tf_op jit(solution)/shard_map/dot_general | solution.py:211
  109.5 15.9 %fusion.96 = (f32[2,1016]{1,0:T(2,128)S(1)}, f32[2,1016,3064]{2,1,0:T(8,128)}) fusion(pred[1016,3064]{1,0:T(8,128)(4,1)} %fusion.4, bf16[1016,128]{1,0:T(8,128)(2,1)S(1)} %copy.49, bf16[2048,128]{1,0:T(8,128)(2,1)S(1)} %bitcast.175, bf16[1024,2,64]{2,0,1:T(8,128)(2,1)S(1)} %get-tuple-element.14, bf16[1024,2,64]{2,0,1:T(8,128)(2,1)S(1)} %get-tuple-element.15), kind=kOutput, calls=%fused_computation.188 | convolution fusion | flops 1621384704 | bytes 29334016 | tf_op jit(solution)/shard_map/sub | solution.py:48
  125.4 12.3 %fusion.32 = bf16[1016,2,128]{2,0,1:T(8,128)(2,1)S(1)} fusion(f32[2,1016,3064]{2,1,0:T(8,128)} %get-tuple-element.31, f32[2,1016]{1,0:T(2,128)S(1)} %get-tuple-element.30, bf16[1016,128]{1,0:T(8,128)(2,1)S(1)} %slice.142, bf16[2048,128]{1,0:T(8,128)(2,1)S(1)} %bitcast.176), kind=kOutput, calls=%fused_computation.50 | convolution fusion | flops 1608149248 | bytes 26216896 | tf_op jit(solution)/shard_map/gck,kd->cgd/dot_general | solution.py:50
  137.8 20.7 %all-to-all-done.1 = bf16[8,256,2048]{2,1,0:T(8,128)(2,1)} async-done(((bf16[8,256,2048]{2,1,0:T(8,128)(2,1)}), bf16[8,256,2048]{2,1,0:T(8,128)(2,1)}, u32[]{:S(2)}, u32[]{:S(2)}) %all-to-all-start.1) | async-done | bytes 8388640 | tf_op jit(solution)/shard_map/all_to_all | solution.py:187
  158.4 12.4 %all-gather.5.cloned.1.call-done = bf16[3,768,2048]{2,1,0:T(8,128)(2,1)} async-done(((bf16[3,48,2048]{2,1,0:T(8,128)(2,1)}), bf16[3,768,2048]{2,1,0:T(8,128)(2,1)}) %all-gather.5.cloned.1.call-update) | async-done | bytes 9437200 | tf_op jit(solution)/shard_map/all_gather | solution.py:203
  171.9 33.3 %all-gather.7.cloned.1.call-done = bf16[1024,2048]{0,1:T(8,128)(2,1)} async-done(((bf16[1024,256]{0,1:T(8,128)(2,1)}), bf16[1024,2048]{0,1:T(8,128)(2,1)}) %all-gather.7.cloned.1.call-update) | async-done | bytes 4194320 | tf_op jit(solution)/shard_map/all_gather | solution.py:252
  205.2 14.6 %fusion.7 = (f32[1024]{0:T(1024)S(1)}, bf16[1024,2048]{1,0:T(8,128)(2,1)S(1)}) fusion(bf16[1024,2048]{0,1:T(8,128)(2,1)} %all-gather.7.cloned.1.call-done, bf16[2048,2048]{1,0:T(8,128)(2,1)} %bitcast.25, bf16[1024,2048]{1,0:T(8,128)(2,1)} %all-gather.9.cloned.1.call-done), kind=kOutput, calls=%fused_computation.26 | convolution fusion | flops 8602516480 | bytes 20975616 | tf_op jit(solution)/shard_map/dot_general | solution.py:254
  219.9 7.0 %fusion.18 = f32[1024,768]{1,0:T(8,128)S(1)} fusion(bf16[3,768,2048]{2,1,0:T(8,128)(2,1)} %all-gather.5.cloned.1.call-done, bf16[1024,2048]{1,0:T(8,128)(2,1)S(1)} %get-tuple-element.33, f32[2048]{0:T(1024)S(1)} %copy-done.17, f32[1024]{0:T(1024)S(1)} %add_rsqrt_fusion.1), kind=kOutput, calls=%fused_computation.37 | convolution fusion | flops 3229614080 | bytes 10498048 | tf_op jit(solution)/shard_map/dot_general | solution.py:259
  227.0 3.9 %multiply_convert_fusion = bf16[1024,768]{1,0:T(8,128)(2,1)S(1)} fusion(f32[1024,768]{1,0:T(8,128)S(1)} %fusion.18, bf16[3,768,2048]{2,1,0:T(8,128)(2,1)S(1)} %bitcast.145, bf16[1024,2048]{1,0:T(8,128)(2,1)S(1)} %get-tuple-element.33, f32[2048]{0:T(1024)S(1)} %copy-done.17, f32[1024]{0:T(1024)S(1)} %add_rsqrt_fusion.1), kind=kOutput, calls=%fused_computation.41 | convolution fusion | flops 3234332672 | bytes 12070912 | tf_op jit(solution)/shard_map/dot_general | solution.py:258
  230.9 5.6 %fusion.16 = f32[1024,2048]{1,0:T(8,128)} fusion(bf16[1024,768]{1,0:T(8,128)(2,1)S(1)} %multiply_convert_fusion, bf16[3,768,2048]{2,1,0:T(8,128)(2,1)S(1)} %bitcast.145), kind=kOutput, calls=%fused_computation.35 | convolution fusion | flops 3221225472 | bytes 13107200 | tf_op jit(solution)/shard_map/dot_general | solution.py:263
  244.6 6.2 %collective-permute-done.3 = f32[16,2048]{1,0:T(8,128)S(1)} collective-permute-done((f32[16,2048]{1,0:T(8,128)S(1)}, f32[16,2048]{1,0:T(8,128)S(1)}, u32[]{:S(2)}, u32[]{:S(2)}) %collective-permute-start.3) | collective-permute-done | bytes 131104 | tf_op jit(solution)/shard_map/ppermute | solution.py:106
  261.8 2.7 collective-permute-start.9
  265.3 3.3 collective-permute-done.9
  271.2 4.3 %convolution_reduce_fusion = f32[144]{0:T(256)S(1)} fusion(bf16[144,2048]{1,0:T(8,128)(2,1)S(1)} %reshape.484, bf16[2048,1187]{0,1:T(8,128)(2,1)} %param.41), kind=kOutput, calls=%fused_computation.52 | convolution fusion | flops 700291840 | bytes 5452352 | tf_op jit(solution)/shard_map/dot_general | solution.py:272
  275.4 5.0 %collective-permute-start.10 = (f32[144]{0:T(256)S(1)}, f32[144]{0:T(256)S(1)}, u32[]{:S(2)}, u32[]{:S(2)}) collective-permute-start(f32[144]{0:T(256)S(1)} %convolution_reduce_fusion), channel_id=1, source_target_pairs={{0,1},{1,0},{2,3},{3,2},{4,5},{5,4},{6,7},{7,6},{8,9},{9,8},{10,11... | collective-permute-start | bytes 1736 | tf_op jit(solution)/shard_map/ppermute | solution.py:106
  303.1 23.8 %all_to_all.29 = bf16[128,2,1024]{2,1,0:T(2,128)(2,1)S(1)} all-to-all(bf16[128,2,1024]{2,1,0:T(2,128)(2,1)S(1)} %reshape.576), channel_id=1, replica_groups=mesh['req'=16,'kv'=8] {'req','kv'}, dimensions={0} | all-to-all | bytes 1048576 | tf_op jit(solution)/shard_map/all_to_all | solution.py:147
  (184 shorter events, 75.7 us)
Async XLA Ops:
  13.5 25.2 %all-to-all-start = ((bf16[128,2,1024]{2,1,0:T(2,128)(2,1)}), bf16[128,2,1024]{2,1,0:T(2,128)(2,1)S(1)}, u32[]{:S(2)}, u32[]{:S(2)}) async-start(bf16[128,2,1024]{2,1,0:T(2,128)(2,1)} %reshape.574), calls=%async_computation | async-start | bytes 1048576 | tf_op jit(solution)/shard_map/all_to_all | solution.py:147
  25.0 61.6 %all-gather.9.cloned.1.call-start = ((), (), s32[]{:S(2)}) async-start(), calls=%async_computation.7 | async-start | bytes 4718592 | tf_op jit(solution)/shard_map/all_gather | solution.py:185
  41.3 129.5 %all-gather.5.cloned.1.call-start = ((), (), s32[]{:S(2)}) async-start(), calls=%async_computation.4 | async-start | bytes 10027008 | tf_op jit(solution)/shard_map/all_gather | solution.py:203
  50.2 108.2 %all-to-all-start.1 = ((bf16[8,256,2048]{2,1,0:T(8,128)(2,1)}), bf16[8,256,2048]{2,1,0:T(8,128)(2,1)}, u32[]{:S(2)}, u32[]{:S(2)}) async-start(bf16[8,256,2048]{2,1,0:T(8,128)(2,1)} %broadcast_in_dim.46), calls=%async_computation.1 | async-start | bytes 16777216 | tf_op jit(solution)/shard_map/all_to_all | solution.py:187
  56.1 149.1 %all-gather.7.cloned.1.call-start = ((), (), s32[]{:S(2)}) async-start(), calls=%async_computation.5 | async-start | bytes 4718592 | tf_op jit(solution)/shard_map/all_gather | solution.py:252
  171.9 127.5 %reduce-scatter.2.cloned.1.call-start = ((), (), s32[]{:S(2)}) async-start(), calls=%async_computation.6 | async-start | bytes 9437184 | tf_op jit(solution)/shard_map/reduce_scatter | solution.py:264
  241.2 9.6 %collective-permute-start.3 = (f32[16,2048]{1,0:T(8,128)S(1)}, f32[16,2048]{1,0:T(8,128)S(1)}, u32[]{:S(2)}, u32[]{:S(2)}) collective-permute-start(f32[16,2048]{1,0:T(8,128)S(1)} %fusion.116), channel_id=1, source_target_pairs={{0,6},{1,7},{2,4},{3,5},{4,2},{5,3},{6,0},{7,1},{8,14},{9,15},{10,... | collective-permute-start | bytes 393224 | tf_op jit(solution)/shard_map/ppermute | solution.py:106
  241.8 8.9 %collective-permute-start.2 = (f32[16,2048]{1,0:T(8,128)S(1)}, f32[16,2048]{1,0:T(8,128)S(1)}, u32[]{:S(2)}, u32[]{:S(2)}) collective-permute-start(f32[16,2048]{1,0:T(8,128)S(1)} %fusion.116), channel_id=1, source_target_pairs={{0,4},{1,5},{2,6},{3,7},{4,0},{5,1},{6,2},{7,3},{8,12},{9,13},{10,... | collective-permute-start | bytes 393224 | tf_op jit(solution)/shard_map/ppermute | solution.py:106
  243.2 8.9 %collective-permute-start.1 = (f32[16,2048]{1,0:T(8,128)S(1)}, f32[16,2048]{1,0:T(8,128)S(1)}, u32[]{:S(2)}, u32[]{:S(2)}) collective-permute-start(f32[16,2048]{1,0:T(8,128)S(1)} %fusion.116), channel_id=1, source_target_pairs={{0,2},{1,3},{2,0},{3,1},{4,6},{5,7},{6,4},{7,5},{8,10},{9,11},{10,... | collective-permute-start | bytes 393224 | tf_op jit(solution)/shard_map/ppermute | solution.py:106
  253.9 4.8 %collective-permute-start.6 = (bf16[9,2048]{1,0:T(8,128)(2,1)S(1)}, bf16[9,2048]{1,0:T(8,128)(2,1)S(1)}, u32[]{:S(2)}, u32[]{:S(2)}) collective-permute-start(bf16[9,2048]{1,0:T(8,128)(2,1)S(1)} %fusion.56), channel_id=1, source_target_pairs={{0,24},{8,16},{16,8},{24,0},{32,56},{40,48},{48,40},{56,32},{64,88... | collective-permute-start | bytes 110600 | tf_op jit(solution)/shard_map/ppermute | solution.py:106
  256.4 4.7 %collective-permute-start.5 = (bf16[9,2048]{1,0:T(8,128)(2,1)S(1)}, bf16[9,2048]{1,0:T(8,128)(2,1)S(1)}, u32[]{:S(2)}, u32[]{:S(2)}) collective-permute-start(bf16[9,2048]{1,0:T(8,128)(2,1)S(1)} %fusion.56), channel_id=1, source_target_pairs={{0,16},{8,24},{16,0},{24,8},{32,48},{40,56},{48,32},{56,40},{64,80... | collective-permute-start | bytes 110600 | tf_op jit(solution)/shard_map/ppermute | solution.py:106
  257.0 4.2 %collective-permute-start.4 = (bf16[9,2048]{1,0:T(8,128)(2,1)S(1)}, bf16[9,2048]{1,0:T(8,128)(2,1)S(1)}, u32[]{:S(2)}, u32[]{:S(2)}) collective-permute-start(bf16[9,2048]{1,0:T(8,128)(2,1)S(1)} %fusion.56), channel_id=1, source_target_pairs={{0,8},{8,0},{16,24},{24,16},{32,40},{40,32},{48,56},{56,48},{64,72... | collective-permute-start | bytes 110600 | tf_op jit(solution)/shard_map/ppermute | solution.py:106
  261.8 6.8 %collective-permute-start.9 = (bf16[36,2048]{1,0:T(8,128)(2,1)S(1)}, bf16[36,2048]{1,0:T(8,128)(2,1)S(1)}, u32[]{:S(2)}, u32[]{:S(2)}) collective-permute-start(bf16[36,2048]{1,0:T(8,128)(2,1)S(1)} %reshape.483), channel_id=1, source_target_pairs={{0,96},{8,104},{16,112},{24,120},{32,64},{40,72},{48,80},{56,88},{... | collective-permute-start | bytes 442376 | tf_op jit(solution)/shard_map/ppermute | solution.py:106
  264.6 5.7 %collective-permute-start.8 = (bf16[36,2048]{1,0:T(8,128)(2,1)S(1)}, bf16[36,2048]{1,0:T(8,128)(2,1)S(1)}, u32[]{:S(2)}, u32[]{:S(2)}) collective-permute-start(bf16[36,2048]{1,0:T(8,128)(2,1)S(1)} %reshape.483), channel_id=1, source_target_pairs={{0,64},{8,72},{16,80},{24,88},{32,96},{40,104},{48,112},{56,120},{... | collective-permute-start | bytes 442376 | tf_op jit(solution)/shard_map/ppermute | solution.py:106
  265.0 5.3 %collective-permute-start.7 = (bf16[36,2048]{1,0:T(8,128)(2,1)S(1)}, bf16[36,2048]{1,0:T(8,128)(2,1)S(1)}, u32[]{:S(2)}, u32[]{:S(2)}) collective-permute-start(bf16[36,2048]{1,0:T(8,128)(2,1)S(1)} %reshape.483), channel_id=1, source_target_pairs={{0,32},{8,40},{16,48},{24,56},{32,0},{40,8},{48,16},{56,24},{64,96... | collective-permute-start | bytes 442376 | tf_op jit(solution)/shard_map/ppermute | solution.py:106
  275.4 5.8 %collective-permute-start.10 = (f32[144]{0:T(256)S(1)}, f32[144]{0:T(256)S(1)}, u32[]{:S(2)}, u32[]{:S(2)}) collective-permute-start(f32[144]{0:T(256)S(1)} %convolution_reduce_fusion), channel_id=1, source_target_pairs={{0,1},{1,0},{2,3},{3,2},{4,5},{5,4},{6,7},{7,6},{8,9},{9,8},{10,11... | collective-permute-start | bytes 1736 | tf_op jit(solution)/shard_map/ppermute | solution.py:106
  281.8 4.2 %collective-permute-start.13 = (f32[144]{0:T(256)S(1)}, f32[144]{0:T(256)S(1)}, u32[]{:S(2)}, u32[]{:S(2)}) collective-permute-start(f32[144]{0:T(256)S(1)} %bitcast.167), channel_id=1, source_target_pairs={{0,6},{1,7},{2,4},{3,5},{4,2},{5,3},{6,0},{7,1},{8,14},{9,15},{10,... | collective-permute-start | bytes 1736 | tf_op jit(solution)/shard_map/ppermute | solution.py:106
  282.0 4.0 %collective-permute-start.12 = (f32[144]{0:T(256)S(1)}, f32[144]{0:T(256)S(1)}, u32[]{:S(2)}, u32[]{:S(2)}) collective-permute-start(f32[144]{0:T(256)S(1)} %bitcast.168), channel_id=1, source_target_pairs={{0,4},{1,5},{2,6},{3,7},{4,0},{5,1},{6,2},{7,3},{8,12},{9,13},{10,... | collective-permute-start | bytes 1736 | tf_op jit(solution)/shard_map/ppermute | solution.py:106
  287.6 3.7 %collective-permute-start.16 = (f32[144]{0:T(256)S(1)}, f32[144]{0:T(256)S(1)}, u32[]{:S(2)}, u32[]{:S(2)}) collective-permute-start(f32[144]{0:T(256)S(1)} %bitcast.163), channel_id=1, source_target_pairs={{0,24},{8,16},{16,8},{24,0},{32,56},{40,48},{48,40},{56,32},{64,88... | collective-permute-start | bytes 1736 | tf_op jit(solution)/shard_map/ppermute | solution.py:106
  288.8 3.9 %collective-permute-start.15 = (f32[144]{0:T(256)S(1)}, f32[144]{0:T(256)S(1)}, u32[]{:S(2)}, u32[]{:S(2)}) collective-permute-start(f32[144]{0:T(256)S(1)} %bitcast.164), channel_id=1, source_target_pairs={{0,16},{8,24},{16,0},{24,8},{32,48},{40,56},{48,32},{56,40},{64,80... | collective-permute-start | bytes 1736 | tf_op jit(solution)/shard_map/ppermute | solution.py:106
  289.5 3.2 collective-permute-start.14
  292.7 3.7 %collective-permute-start.19 = (f32[144]{0:T(256)S(1)}, f32[144]{0:T(256)S(1)}, u32[]{:S(2)}, u32[]{:S(2)}) collective-permute-start(f32[144]{0:T(256)S(1)} %maximum_maximum_fusion.1), channel_id=1, source_target_pairs={{0,96},{8,104},{16,112},{24,120},{32,64},{40,72},{48,80},{56,88},{... | collective-permute-start | bytes 1736 | tf_op jit(solution)/shard_map/ppermute | solution.py:106
  294.9 3.9 %collective-permute-start.18 = (f32[144]{0:T(256)S(1)}, f32[144]{0:T(256)S(1)}, u32[]{:S(2)}, u32[]{:S(2)}) collective-permute-start(f32[144]{0:T(256)S(1)} %maximum_maximum_fusion.1), channel_id=1, source_target_pairs={{0,64},{8,72},{16,80},{24,88},{32,96},{40,104},{48,112},{56,120},{... | collective-permute-start | bytes 1736 | tf_op jit(solution)/shard_map/ppermute | solution.py:106
  295.2 3.5 %collective-permute-start.17 = (f32[144]{0:T(256)S(1)}, f32[144]{0:T(256)S(1)}, u32[]{:S(2)}, u32[]{:S(2)}) collective-permute-start(f32[144]{0:T(256)S(1)} %maximum_maximum_fusion.1), channel_id=1, source_target_pairs={{0,32},{8,40},{16,48},{24,56},{32,0},{40,8},{48,16},{56,24},{64,96... | collective-permute-start | bytes 1736 | tf_op jit(solution)/shard_map/ppermute | solution.py:106
  (23 other events, 285.9 us)
Sparse Core Ops, SparseCore 0:
  41.4 45.1 all-gather.8
  88.7 82.0 all-gather.4
  173.1 32.0 all-gather.6
  236.7 55.1 reduce-scatter.1
where the time goes:
time: 341 us; the launch traced here: 336 us
  waiting for transfers between devices  127 us (37%)
  matrix products  78.2 us (23%)
  starting transfers between devices  43.1 us (13%)
  local copies, waits for them, and re-layouts  26.2 us (8%)
  blocking collectives  23.8 us (7%)
  other arithmetic  22.4 us (7%)
  between operations  15.3 us (4%)
    all_gather x1, waiting for transfers between devices, shards(): lax.all_gather(pieces.reshape(tok_req, q_cols), 'kv', axis=1, tiled=True)  33.3 us
    ppermute x20, starting transfers between devices, radix_exchange(): got.append(lax.ppermute(value, axis, pairs))  25.5 us
    ppermute x20, waiting for transfers between devices, radix_exchange(): got.append(lax.ppermute(value, axis, pairs))  24.5 us
    all_to_all x1, blocking collectives, regroup(): lax.all_to_all(rows_in, ('req', 'kv'), split_axis=0, concat_axis=0, tiled...  23.8 us
    all_gather x1, waiting for transfers between devices, shards(): rows_all = lax.all_gather(owner_rows, 'kv', axis=0, tiled=True)  23.5 us
    all_to_all x1, waiting for transfers between devices, shards(): lax.all_to_all(jnp.broadcast_to(o_proj[None], (kv_count,) + o_proj.shape)...  20.7 us
    sub x1, matrix products, prefill_full(): expd = jnp.exp(scores - row_peak)  15.9 us
    dot_general x1, matrix products, shards(): jnp.dot(attended, o_full, preferred_element_type=jnp.float32)  14.6 us
  transfers between devices with their start and end apart: 26, of which 19 were waited for; matrix products, arithmetic and copies ran while one was open for 23% of the time, Pallas kernels for 0%

commit v1 on v0

--- a/solution.py
+++ b/solution.py
@@ -5,6 +5,13 @@
 
 EPS = 1e-06
 NEG = -1e30
+
+
+def exchange_gather(shard, mesh_axis, dim):
+    size = lax.axis_size(mesh_axis)
+    blocks = jnp.stack([shard for _ in range(size)])
+    blocks = lax.all_to_all(blocks, mesh_axis, split_axis=0, concat_axis=0)
+    return jnp.concatenate(blocks, axis=dim)
 
 
 def spread(value, axis, root):
@@ -182,7 +189,7 @@
     slot_place = lax.dynamic_index_in_dim(slot_table, self_index, 0, keepdims=False) // rows_dev
     arrived = regroup(hidden_in[send_rows])
     owner_rows = arrived[slot_place]
-    rows_all = lax.all_gather(owner_rows, "kv", axis=0, tiled=True)
+    rows_all = exchange_gather(owner_rows, "kv", 0)
     normed = norm_rows(rows_all, attn_gain).astype(jnp.bfloat16)
     o_full = lax.all_to_all(
         jnp.broadcast_to(o_proj[None], (kv_count,) + o_proj.shape),

time: 341 us -> 372 us (1.091)
  waiting for transfers between devices: 127 us -> 149 us
  starting transfers between devices: 43.1 us -> 48.4 us
    all_to_all x0 -> x1, waiting for transfers between devices: none -> 41.6 us  [exchange_gather(): blocks = lax.all_to_all(blocks, mesh_axis, split_axis=0, concat_axis=0)]
    all_gather x1 -> x0, waiting for transfers between devices: 23.5 us -> none  [shards(): rows_all = lax.all_gather(owner_rows, 'kv', axis=0, tiled=True)]
    all_to_all x1, waiting for transfers between devices: 20.7 us -> 41.1 us  [shards(): lax.all_to_all(jnp.broadcast_to(o_proj[None], (kv_count,) + o_proj.shape)...]
    all_gather x1, waiting for transfers between devices: 12.4 us -> 0.01 us  [shards(): weight_all = lax.all_gather(weight_piece, 'req', axis=1, tiled=True)]
    convert_element_type x1 -> x2, other arithmetic: 1.01 us -> 6.59 us  [shards(): normed = norm_rows(rows_all, attn_gain).astype(jnp.bfloat16)]
    all_to_all x0 -> x1, starting transfers between devices: none -> 5.45 us  [exchange_gather(): blocks = lax.all_to_all(blocks, mesh_axis, split_axis=0, concat_axis=0)]
    all_gather x1, waiting for transfers between devices: 33.3 us -> 28.2 us  [shards(): lax.all_gather(pieces.reshape(tok_req, q_cols), 'kv', axis=1, tiled=True)]
    unnamed x49 -> x53, local copies, waits for them, and re-layouts: 4.74 us -> 7.63 us
  transfers between devices with their start and end apart: 26 -> 26, of which waited for: 19 -> 18; matrix products, arithmetic and copies ran while one was open for 23% -> 22% of each run, Pallas kernels for 0% -> 0%
where the time goes in v1:
time: 372 us; the launch traced here: 365 us
  waiting for transfers between devices  149 us (40%)
  matrix products  75.7 us (20%)
  starting transfers between devices  48.4 us (13%)
  local copies, waits for them, and re-layouts  28.1 us (8%)
  other arithmetic  24.7 us (7%)
  blocking collectives  23.8 us (6%)
  between operations  15.3 us (4%)
    all_to_all x1, waiting for transfers between devices, exchange_gather(): blocks = lax.all_to_all(blocks, mesh_axis, split_axis=0, concat_axis=0)  41.6 us
    all_to_all x1, waiting for transfers between devices, shards(): lax.all_to_all(jnp.broadcast_to(o_proj[None], (kv_count,) + o_proj.shape)...  41.1 us
    all_gather x1, waiting for transfers between devices, shards(): lax.all_gather(pieces.reshape(tok_req, q_cols), 'kv', axis=1, tiled=True)  28.2 us
    ppermute x20, starting transfers between devices, radix_exchange(): got.append(lax.ppermute(value, axis, pairs))  25.5 us
    ppermute x20, waiting for transfers between devices, radix_exchange(): got.append(lax.ppermute(value, axis, pairs))  24.6 us
    all_to_all x1, blocking collectives, regroup(): lax.all_to_all(rows_in, ('req', 'kv'), split_axis=0, concat_axis=0, tiled...  23.8 us
    sub x1, matrix products, prefill_full(): expd = jnp.exp(scores - row_peak)  15.5 us
    dot_general x1, matrix products, shards(): jnp.dot(attended, o_full, preferred_element_type=jnp.float32)  14.5 us
  transfers between devices with their start and end apart: 26, of which 18 were waited for; matrix products, arithmetic and copies ran while one was open for 22% of the time, Pallas kernels for 0%

profile of v1, /device:TPU:1, one launch (start us, length us, event | category | flops | bytes accessed | tf_op | source)
XLA Modules:
  0.0 365.1 jit_solution(3081207927116564256)
XLA Ops:
  15.6 11.5 %all-to-all-start = ((bf16[128,2,1024]{2,1,0:T(2,128)(2,1)}), bf16[128,2,1024]{2,1,0:T(2,128)(2,1)S(1)}, u32[]{:S(2)}, u32[]{:S(2)}) async-start(bf16[128,2,1024]{2,1,0:T(2,128)(2,1)} %reshape.597), calls=%async_computation | async-start | bytes 1048576 | tf_op jit(solution)/shard_map/all_to_all | solution.py:154
  27.2 13.7 %all-to-all-done = bf16[128,2,1024]{2,1,0:T(2,128)(2,1)S(1)} async-done(((bf16[128,2,1024]{2,1,0:T(2,128)(2,1)}), bf16[128,2,1024]{2,1,0:T(2,128)(2,1)S(1)}, u32[]{:S(2)}, u32[]{:S(2)}) %all-to-all-start) | async-done | bytes 524320 | tf_op jit(solution)/shard_map/all_to_all | solution.py:154
  45.2 5.4 %all-to-all-start.1 = ((bf16[8,128,2048]{2,1,0:T(8,128)(2,1)}), bf16[8,128,2048]{2,1,0:T(8,128)(2,1)}, u32[]{:S(2)}, u32[]{:S(2)}) async-start(bf16[8,128,2048]{2,1,0:T(8,128)(2,1)} %stack.92), calls=%async_computation.1 | async-start | bytes 8388608 | tf_op jit(solution)/shard_map/all_to_all | solution.py:13
  53.9 4.1 %fusion.4 = pred[1016,3064]{1,0:T(8,128)(4,1)} fusion(s32[3064]{0:T(1024)S(1)} %iota_add_fusion, pred[3064]{0:T(1024)(128)(4,1)S(1)} %get-tuple-element.36, pred[3064]{0:T(1024)(128)(4,1)S(1)} %get-tuple-element.37), kind=kLoop, calls=%fused_computation.18 | loop fusion | flops 6226048 | bytes 3131408 | tf_op jit(solution)/shard_map/jit(_where)/select_n | solution.py:52
  58.0 41.6 %all-to-all-done.1 = bf16[8,128,2048]{2,1,0:T(8,128)(2,1)} async-done(((bf16[8,128,2048]{2,1,0:T(8,128)(2,1)}), bf16[8,128,2048]{2,1,0:T(8,128)(2,1)}, u32[]{:S(2)}, u32[]{:S(2)}) %all-to-all-start.1) | async-done | bytes 4194336 | tf_op jit(solution)/shard_map/all_to_all | solution.py:13
  99.5 4.4 %broadcast_in_dim.46 = bf16[8,256,2048]{2,1,0:T(8,128)(2,1)} broadcast(bf16[256,2048]{1,0:T(8,128)(2,1)S(1)} %copy-done.5), dimensions={1,2} | broadcast | bytes 9437184 | tf_op jit(solution)/shard_map/broadcast_in_dim | solution.py:195
  103.9 5.7 %all-to-all-start.2 = ((bf16[8,256,2048]{2,1,0:T(8,128)(2,1)}), bf16[8,256,2048]{2,1,0:T(8,128)(2,1)}, u32[]{:S(2)}, u32[]{:S(2)}) async-start(bf16[8,256,2048]{2,1,0:T(8,128)(2,1)} %broadcast_in_dim.46), calls=%async_computation.2 | async-start | bytes 16777216 | tf_op jit(solution)/shard_map/all_to_all | solution.py:194
  112.9 3.3 fusion.12
  118.1 3.3 fusion.14
  126.7 3.5 fusion.90
  130.8 3.7 %convolution_convert_fusion = bf16[1024,128]{1,0:T(8,128)(2,1)S(1)} fusion(bf16[1024,2048]{1,0:T(8,128)(2,1)} %copy-done.3, bf16[2048,128]{1,0:T(8,128)(2,1)} %param.32), kind=kOutput, calls=%fused_computation.54 | convolution fusion | flops 537001984 | bytes 4980736 | tf_op jit(solution)/shard_map/dot_general | solution.py:218
  135.4 15.5 %fusion.91 = (f32[2,1016]{1,0:T(2,128)S(1)}, f32[2,1016,3064]{2,1,0:T(8,128)}) fusion(pred[1016,3064]{1,0:T(8,128)(4,1)} %fusion.4, bf16[1016,128]{1,0:T(8,128)(2,1)S(1)} %copy.52, bf16[2048,128]{1,0:T(8,128)(2,1)S(1)} %bitcast.193, bf16[1024,2,64]{0,2,1:T(8,128)(2,1)S(1)} %get-tuple-element.15, bf16[1024,2,64]{0,2,1:T(8,128)(2,1)S(1)} %get-tuple-element.14), kind=kOutput, calls=%fused_computation.187 | convolution fusion | flops 1621384704 | bytes 29334016 | tf_op jit(solution)/shard_map/sub | solution.py:55
  150.8 11.6 %fusion.34 = bf16[1016,2,128]{2,0,1:T(8,128)(2,1)S(1)} fusion(f32[2,1016,3064]{2,1,0:T(8,128)} %get-tuple-element.33, f32[2,1016]{1,0:T(2,128)S(1)} %get-tuple-element.32, bf16[1016,128]{1,0:T(8,128)(2,1)S(1)} %slice.142, bf16[2048,128]{1,0:T(8,128)(2,1)S(1)} %bitcast.194), kind=kOutput, calls=%fused_computation.53 | convolution fusion | flops 1608149248 | bytes 26216896 | tf_op jit(solution)/shard_map/gck,kd->cgd/dot_general | solution.py:57
  162.4 41.1 %all-to-all-done.2 = bf16[8,256,2048]{2,1,0:T(8,128)(2,1)} async-done(((bf16[8,256,2048]{2,1,0:T(8,128)(2,1)}), bf16[8,256,2048]{2,1,0:T(8,128)(2,1)}, u32[]{:S(2)}, u32[]{:S(2)}) %all-to-all-start.2) | async-done | bytes 8388640 | tf_op jit(solution)/shard_map/all_to_all | solution.py:194
  204.6 28.2 %all-gather.5.cloned.1.call-done = bf16[1024,2048]{0,1:T(8,128)(2,1)} async-done(((bf16[1024,256]{0,1:T(8,128)(2,1)}), bf16[1024,2048]{0,1:T(8,128)(2,1)}) %all-gather.5.cloned.1.call-update) | async-done | bytes 4194320 | tf_op jit(solution)/shard_map/all_gather | solution.py:259
  232.9 14.5 %fusion.7 = (f32[1024]{0:T(1024)S(1)}, bf16[1024,2048]{1,0:T(8,128)(2,1)S(1)}) fusion(bf16[1024,2048]{0,1:T(8,128)(2,1)} %all-gather.5.cloned.1.call-done, bf16[2048,2048]{1,0:T(8,128)(2,1)} %bitcast.30, bf16[8,128,2048]{2,1,0:T(8,128)(2,1)} %all-to-all-done.1), kind=kOutput, calls=%fused_computation.23 | convolution fusion | flops 8602516480 | bytes 20975616 | tf_op jit(solution)/shard_map/dot_general | solution.py:261
  247.4 7.0 %fusion.20 = f32[1024,768]{1,0:T(8,128)S(1)} fusion(bf16[3,768,2048]{2,1,0:T(8,128)(2,1)} %all-gather.3.cloned.1.call-done, bf16[1024,2048]{1,0:T(8,128)(2,1)S(1)} %get-tuple-element.35, f32[2048]{0:T(1024)S(1)} %copy-done.19, f32[1024]{0:T(1024)S(1)} %add_rsqrt_fusion.1), kind=kOutput, calls=%fused_computation.40 | convolution fusion | flops 3229614080 | bytes 10498048 | tf_op jit(solution)/shard_map/dot_general | solution.py:266
  254.5 3.9 %multiply_convert_fusion = bf16[1024,768]{1,0:T(8,128)(2,1)S(1)} fusion(f32[1024,768]{1,0:T(8,128)S(1)} %fusion.20, bf16[3,768,2048]{2,1,0:T(8,128)(2,1)S(1)} %bitcast.162, bf16[1024,2048]{1,0:T(8,128)(2,1)S(1)} %get-tuple-element.35, f32[2048]{0:T(1024)S(1)} %copy-done.19, f32[1024]{0:T(1024)S(1)} %add_rsqrt_fusion.1), kind=kOutput, calls=%fused_computation.44 | convolution fusion | flops 3234332672 | bytes 12070912 | tf_op jit(solution)/shard_map/dot_general | solution.py:265
  259.6 5.6 %fusion.18 = f32[1024,2048]{1,0:T(8,128)} fusion(bf16[1024,768]{1,0:T(8,128)(2,1)S(1)} %multiply_convert_fusion, bf16[3,768,2048]{2,1,0:T(8,128)(2,1)S(1)} %bitcast.162), kind=kOutput, calls=%fused_computation.38 | convolution fusion | flops 3221225472 | bytes 13107200 | tf_op jit(solution)/shard_map/dot_general | solution.py:270
  273.2 6.2 %collective-permute-done.3 = f32[16,2048]{1,0:T(8,128)S(1)} collective-permute-done((f32[16,2048]{1,0:T(8,128)S(1)}, f32[16,2048]{1,0:T(8,128)S(1)}, u32[]{:S(2)}, u32[]{:S(2)}) %collective-permute-start.3) | collective-permute-done | bytes 131104 | tf_op jit(solution)/shard_map/ppermute | solution.py:113
  294.1 3.3 collective-permute-done.9
  299.9 4.3 %convolution_reduce_fusion = f32[144]{0:T(256)S(1)} fusion(bf16[144,2048]{1,0:T(8,128)(2,1)S(1)} %reshape.506, bf16[2048,1187]{0,1:T(8,128)(2,1)} %param.41), kind=kOutput, calls=%fused_computation.55 | convolution fusion | flops 700291840 | bytes 5452352 | tf_op jit(solution)/shard_map/dot_general | solution.py:279
  304.2 5.0 %collective-permute-start.10 = (f32[144]{0:T(256)S(1)}, f32[144]{0:T(256)S(1)}, u32[]{:S(2)}, u32[]{:S(2)}) collective-permute-start(f32[144]{0:T(256)S(1)} %convolution_reduce_fusion), channel_id=1, source_target_pairs={{0,1},{1,0},{2,3},{3,2},{4,5},{5,4},{6,7},{7,6},{8,9},{9,8},{10,11... | collective-permute-start | bytes 1736 | tf_op jit(solution)/shard_map/ppermute | solution.py:113
  331.7 23.8 %all_to_all.34 = bf16[128,2,1024]{2,1,0:T(2,128)(2,1)S(1)} all-to-all(bf16[128,2,1024]{2,1,0:T(2,128)(2,1)S(1)} %reshape.599), channel_id=1, replica_groups=mesh['req'=16,'kv'=8] {'req','kv'}, dimensions={0} | all-to-all | bytes 1048576 | tf_op jit(solution)/shard_map/all_to_all | solution.py:154
  (190 shorter events, 79.7 us)
Async XLA Ops:
  7.2 196.3 %all-gather.3.cloned.1.call-start = ((), (), s32[]{:S(2)}) async-start(), calls=%async_computation.5 | async-start | bytes 10027008 | tf_op jit(solution)/shard_map/all_gather | solution.py:210
  15.6 25.2 %all-to-all-start = ((bf16[128,2,1024]{2,1,0:T(2,128)(2,1)}), bf16[128,2,1024]{2,1,0:T(2,128)(2,1)S(1)}, u32[]{:S(2)}, u32[]{:S(2)}) async-start(bf16[128,2,1024]{2,1,0:T(2,128)(2,1)} %reshape.597), calls=%async_computation | async-start | bytes 1048576 | tf_op jit(solution)/shard_map/all_to_all | solution.py:154
  45.2 54.4 %all-to-all-start.1 = ((bf16[8,128,2048]{2,1,0:T(8,128)(2,1)}), bf16[8,128,2048]{2,1,0:T(8,128)(2,1)}, u32[]{:S(2)}, u32[]{:S(2)}) async-start(bf16[8,128,2048]{2,1,0:T(8,128)(2,1)} %stack.92), calls=%async_computation.1 | async-start | bytes 8388608 | tf_op jit(solution)/shard_map/all_to_all | solution.py:13
  103.9 99.6 %all-to-all-start.2 = ((bf16[8,256,2048]{2,1,0:T(8,128)(2,1)}), bf16[8,256,2048]{2,1,0:T(8,128)(2,1)}, u32[]{:S(2)}, u32[]{:S(2)}) async-start(bf16[8,256,2048]{2,1,0:T(8,128)(2,1)} %broadcast_in_dim.46), calls=%async_computation.2 | async-start | bytes 16777216 | tf_op jit(solution)/shard_map/all_to_all | solution.py:194
  109.6 123.2 %all-gather.5.cloned.1.call-start = ((), (), s32[]{:S(2)}) async-start(), calls=%async_computation.6 | async-start | bytes 4718592 | tf_op jit(solution)/shard_map/all_gather | solution.py:259
  204.6 123.5 %reduce-scatter.2.cloned.1.call-start = ((), (), s32[]{:S(2)}) async-start(), calls=%async_computation.7 | async-start | bytes 9437184 | tf_op jit(solution)/shard_map/reduce_scatter | solution.py:271
  269.9 9.6 %collective-permute-start.3 = (f32[16,2048]{1,0:T(8,128)S(1)}, f32[16,2048]{1,0:T(8,128)S(1)}, u32[]{:S(2)}, u32[]{:S(2)}) collective-permute-start(f32[16,2048]{1,0:T(8,128)S(1)} %fusion.110), channel_id=1, source_target_pairs={{0,6},{1,7},{2,4},{3,5},{4,2},{5,3},{6,0},{7,1},{8,14},{9,15},{10,... | collective-permute-start | bytes 393224 | tf_op jit(solution)/shard_map/ppermute | solution.py:113
  270.5 9.0 %collective-permute-start.2 = (f32[16,2048]{1,0:T(8,128)S(1)}, f32[16,2048]{1,0:T(8,128)S(1)}, u32[]{:S(2)}, u32[]{:S(2)}) collective-permute-start(f32[16,2048]{1,0:T(8,128)S(1)} %fusion.110), channel_id=1, source_target_pairs={{0,4},{1,5},{2,6},{3,7},{4,0},{5,1},{6,2},{7,3},{8,12},{9,13},{10,... | collective-permute-start | bytes 393224 | tf_op jit(solution)/shard_map/ppermute | solution.py:113
  271.9 8.9 %collective-permute-start.1 = (f32[16,2048]{1,0:T(8,128)S(1)}, f32[16,2048]{1,0:T(8,128)S(1)}, u32[]{:S(2)}, u32[]{:S(2)}) collective-permute-start(f32[16,2048]{1,0:T(8,128)S(1)} %fusion.110), channel_id=1, source_target_pairs={{0,2},{1,3},{2,0},{3,1},{4,6},{5,7},{6,4},{7,5},{8,10},{9,11},{10,... | collective-permute-start | bytes 393224 | tf_op jit(solution)/shard_map/ppermute | solution.py:113
  282.6 4.8 %collective-permute-start.6 = (bf16[9,2048]{1,0:T(8,128)(2,1)S(1)}, bf16[9,2048]{1,0:T(8,128)(2,1)S(1)}, u32[]{:S(2)}, u32[]{:S(2)}) collective-permute-start(bf16[9,2048]{1,0:T(8,128)(2,1)S(1)} %fusion.57), channel_id=1, source_target_pairs={{0,24},{8,16},{16,8},{24,0},{32,56},{40,48},{48,40},{56,32},{64,88... | collective-permute-start | bytes 110600 | tf_op jit(solution)/shard_map/ppermute | solution.py:113
  285.1 4.7 %collective-permute-start.5 = (bf16[9,2048]{1,0:T(8,128)(2,1)S(1)}, bf16[9,2048]{1,0:T(8,128)(2,1)S(1)}, u32[]{:S(2)}, u32[]{:S(2)}) collective-permute-start(bf16[9,2048]{1,0:T(8,128)(2,1)S(1)} %fusion.57), channel_id=1, source_target_pairs={{0,16},{8,24},{16,0},{24,8},{32,48},{40,56},{48,32},{56,40},{64,80... | collective-permute-start | bytes 110600 | tf_op jit(solution)/shard_map/ppermute | solution.py:113
  285.7 4.2 %collective-permute-start.4 = (bf16[9,2048]{1,0:T(8,128)(2,1)S(1)}, bf16[9,2048]{1,0:T(8,128)(2,1)S(1)}, u32[]{:S(2)}, u32[]{:S(2)}) collective-permute-start(bf16[9,2048]{1,0:T(8,128)(2,1)S(1)} %fusion.57), channel_id=1, source_target_pairs={{0,8},{8,0},{16,24},{24,16},{32,40},{40,32},{48,56},{56,48},{64,72... | collective-permute-start | bytes 110600 | tf_op jit(solution)/shard_map/ppermute | solution.py:113
  290.6 6.8 %collective-permute-start.9 = (bf16[36,2048]{1,0:T(8,128)(2,1)S(1)}, bf16[36,2048]{1,0:T(8,128)(2,1)S(1)}, u32[]{:S(2)}, u32[]{:S(2)}) collective-permute-start(bf16[36,2048]{1,0:T(8,128)(2,1)S(1)} %reshape.505), channel_id=1, source_target_pairs={{0,96},{8,104},{16,112},{24,120},{32,64},{40,72},{48,80},{56,88},{... | collective-permute-start | bytes 442376 | tf_op jit(solution)/shard_map/ppermute | solution.py:113
  293.3 5.8 %collective-permute-start.8 = (bf16[36,2048]{1,0:T(8,128)(2,1)S(1)}, bf16[36,2048]{1,0:T(8,128)(2,1)S(1)}, u32[]{:S(2)}, u32[]{:S(2)}) collective-permute-start(bf16[36,2048]{1,0:T(8,128)(2,1)S(1)} %reshape.505), channel_id=1, source_target_pairs={{0,64},{8,72},{16,80},{24,88},{32,96},{40,104},{48,112},{56,120},{... | collective-permute-start | bytes 442376 | tf_op jit(solution)/shard_map/ppermute | solution.py:113
  293.7 5.4 %collective-permute-start.7 = (bf16[36,2048]{1,0:T(8,128)(2,1)S(1)}, bf16[36,2048]{1,0:T(8,128)(2,1)S(1)}, u32[]{:S(2)}, u32[]{:S(2)}) collective-permute-start(bf16[36,2048]{1,0:T(8,128)(2,1)S(1)} %reshape.505), channel_id=1, source_target_pairs={{0,32},{8,40},{16,48},{24,56},{32,0},{40,8},{48,16},{56,24},{64,96... | collective-permute-start | bytes 442376 | tf_op jit(solution)/shard_map/ppermute | solution.py:113
  304.2 5.8 %collective-permute-start.10 = (f32[144]{0:T(256)S(1)}, f32[144]{0:T(256)S(1)}, u32[]{:S(2)}, u32[]{:S(2)}) collective-permute-start(f32[144]{0:T(256)S(1)} %convolution_reduce_fusion), channel_id=1, source_target_pairs={{0,1},{1,0},{2,3},{3,2},{4,5},{5,4},{6,7},{7,6},{8,9},{9,8},{10,11... | collective-permute-start | bytes 1736 | tf_op jit(solution)/shard_map/ppermute | solution.py:113
  310.6 4.2 %collective-permute-start.13 = (f32[144]{0:T(256)S(1)}, f32[144]{0:T(256)S(1)}, u32[]{:S(2)}, u32[]{:S(2)}) collective-permute-start(f32[144]{0:T(256)S(1)} %bitcast.185), channel_id=1, source_target_pairs={{0,6},{1,7},{2,4},{3,5},{4,2},{5,3},{6,0},{7,1},{8,14},{9,15},{10,... | collective-permute-start | bytes 1736 | tf_op jit(solution)/shard_map/ppermute | solution.py:113
  310.7 4.0 %collective-permute-start.12 = (f32[144]{0:T(256)S(1)}, f32[144]{0:T(256)S(1)}, u32[]{:S(2)}, u32[]{:S(2)}) collective-permute-start(f32[144]{0:T(256)S(1)} %bitcast.186), channel_id=1, source_target_pairs={{0,4},{1,5},{2,6},{3,7},{4,0},{5,1},{6,2},{7,3},{8,12},{9,13},{10,... | collective-permute-start | bytes 1736 | tf_op jit(solution)/shard_map/ppermute | solution.py:113
  316.3 3.7 %collective-permute-start.16 = (f32[144]{0:T(256)S(1)}, f32[144]{0:T(256)S(1)}, u32[]{:S(2)}, u32[]{:S(2)}) collective-permute-start(f32[144]{0:T(256)S(1)} %bitcast.181), channel_id=1, source_target_pairs={{0,24},{8,16},{16,8},{24,0},{32,56},{40,48},{48,40},{56,32},{64,88... | collective-permute-start | bytes 1736 | tf_op jit(solution)/shard_map/ppermute | solution.py:113
  317.5 3.9 %collective-permute-start.15 = (f32[144]{0:T(256)S(1)}, f32[144]{0:T(256)S(1)}, u32[]{:S(2)}, u32[]{:S(2)}) collective-permute-start(f32[144]{0:T(256)S(1)} %bitcast.182), channel_id=1, source_target_pairs={{0,16},{8,24},{16,0},{24,8},{32,48},{40,56},{48,32},{56,40},{64,80... | collective-permute-start | bytes 1736 | tf_op jit(solution)/shard_map/ppermute | solution.py:113
  318.2 3.2 collective-permute-start.14
  321.4 3.7 %collective-permute-start.19 = (f32[144]{0:T(256)S(1)}, f32[144]{0:T(256)S(1)}, u32[]{:S(2)}, u32[]{:S(2)}) collective-permute-start(f32[144]{0:T(256)S(1)} %maximum_maximum_fusion.1), channel_id=1, source_target_pairs={{0,96},{8,104},{16,112},{24,120},{32,64},{40,72},{48,80},{56,88},{... | collective-permute-start | bytes 1736 | tf_op jit(solution)/shard_map/ppermute | solution.py:113
  323.6 3.9 %collective-permute-start.18 = (f32[144]{0:T(256)S(1)}, f32[144]{0:T(256)S(1)}, u32[]{:S(2)}, u32[]{:S(2)}) collective-permute-start(f32[144]{0:T(256)S(1)} %maximum_maximum_fusion.1), channel_id=1, source_target_pairs={{0,64},{8,72},{16,80},{24,88},{32,96},{40,104},{48,112},{56,120},{... | collective-permute-start | bytes 1736 | tf_op jit(solution)/shard_map/ppermute | solution.py:113
  323.9 3.5 collective-permute-start.17
  (25 other events, 267.4 us)
Sparse Core Ops, SparseCore 0:
  12.0 84.5 all-gather.2
  204.7 28.1 all-gather.4
  265.3 55.1 reduce-scatter.1
